TPU v7x, 32 devices: a whole 2x2x4 slice. The times are simulated.
32 devices in a mesh: seq: 8 (over z, x), fsdp: 4 (over y, core).
Axes of the slice: x: 2, y: 2, z: 4, core: 2. Of those that a mesh axis runs over, the one named last changes fastest.
Arguments:
- inputs: bfloat16 [4, 1024, 768], P('fsdp', 'seq'), may hold values from -6 to 6
- cotangent: bfloat16 [4, 1024, 768], P('fsdp', 'seq'), may hold values from -6 to 6
- inproj: bfloat16 [1, 768, 3352], P(None, 'fsdp'), may hold values from -0.21875 to 0.21875
- outproj: bfloat16 [1, 1536, 768], P(None, 'fsdp'), may hold values from -0.15625 to 0.15625
- norm_gain: float32 [1, 768], replicated, may hold values from 0.5 to 2
- gate_gain: float32 [1, 1536], replicated, may hold values from 0.5 to 2
- conv_weight: float32 [1, 4, 1792], replicated, may hold values from -3 to 3
- conv_bias: float32 [1, 1792], replicated, may hold values from -0.5 to 0.5
- step_bias: float32 [1, 24], replicated, may hold values from -5.5 to -4.5
- log_rate: float32 [1, 24], replicated, may hold values from -7 to 1.5
- skip_gain: float32 [1, 24], replicated, may hold values from 0.5 to 2
Outputs:
- output: bfloat16 [4, 1024, 768], P('fsdp', 'seq')
- input_grad: bfloat16 [4, 1024, 768], P('fsdp', 'seq')
- inproj_grad: float32 [1, 768, 3352], P(None, 'fsdp')
- outproj_grad: float32 [1, 1536, 768], P(None, 'fsdp')
- norm_grad: float32 [1, 768], replicated
- gate_grad: float32 [1, 1536], replicated
- kernel_grad: float32 [1, 4, 1792], replicated
- bias_grad: float32 [1, 1792], replicated
- step_grad: float32 [1, 24], replicated
- rate_grad: float32 [1, 24], replicated
- skip_grad: float32 [1, 24], replicated
All inputs are finite; a program needn't handle non-finite values.
Results may differ from a plain program's by a relative error of at most 0.01.
Values may be sent and summed in bfloat16 or wider, within the bound.
A program may use at most 192 MiB of HBM per device.

v0:
```python
import jax
import jax.numpy as jnp
from jax import lax
from jax.sharding import PartitionSpec as P

H = 24
P_SIZE = 64
N = 128
CONV = 4
SPAN = 64
LAYERS = 1
DI = 1536
XBC = 1792


epsilon = 1e-05
highest = lax.Precision.HIGHEST


def passed_along(shard, axis, by):
    length = lax.axis_size(axis)
    pairs = [(i, i + by) for i in range(length) if 0 <= i + by < length]
    return lax.ppermute(shard, axis, pairs)


def prefix(shard, axis, combine, identity):
    length, index = (lax.axis_size(axis), lax.axis_index(axis))
    everything = jax.tree.map(
        lambda part, kind: lax.all_gather(part.astype(kind), axis),
        shard,
        (jnp.bfloat16, jnp.bfloat16),
    )
    start = jax.tree.map(
        lambda part, zero: jnp.broadcast_to(jnp.asarray(zero, part.dtype), part.shape),
        shard,
        identity,
    )

    def prefix_step(k, before):
        reached = k < index
        new = combine(
            before, jax.tree.map(lambda part, own: part[k].astype(own.dtype), everything, shard)
        )
        return jax.tree.map(lambda a, b: jnp.where(reached, a, b), new, before)

    return lax.fori_loop(0, length, prefix_step, start)


def carried_in(shard, axis, combine, identity):
    length, index = (lax.axis_size(axis), lax.axis_index(axis))
    everything = jax.tree.map(
        lambda part, kind: lax.all_gather(part.astype(kind), axis),
        shard,
        jax.tree.map(lambda a: jnp.bfloat16 if a.dtype == jnp.float32 else a.dtype, shard),
    )
    start = jax.tree.map(
        lambda part, zero: jnp.broadcast_to(jnp.asarray(zero, part.dtype), part.shape),
        shard,
        identity,
    )

    def carried_step(k, before):
        at = length - 1 - k
        reached = at > index
        new = combine(
            before, jax.tree.map(lambda part, own: part[at].astype(own.dtype), everything, shard)
        )
        return jax.tree.map(lambda a, b: jnp.where(reached, a, b), new, before)

    return lax.fori_loop(0, length, carried_step, start)


def rms_scale(values, gain):
    return values * lax.rsqrt(jnp.mean(values * values, axis=-1, keepdims=True) + epsilon) * gain


def section_one(projected, rim_rows, conv_weight, conv_bias, step_bias, log_rate):
    tokens = projected.shape[0]
    conv_input = projected[:, DI : DI + XBC]
    step_raw = projected[:, DI + XBC :]
    extended = jnp.concatenate([rim_rows, conv_input], axis=0)
    conv_sum = conv_bias + conv_weight[0] * extended[0:tokens]
    for offset in range(1, CONV):
        conv_sum = conv_sum + conv_weight[offset] * extended[offset : offset + tokens]
    conv_act = jax.nn.silu(conv_sum)
    blocks = tokens // SPAN
    head_input = conv_act[:, :DI].reshape(blocks, SPAN, H, P_SIZE)
    in_coeff = conv_act[:, DI : DI + N].reshape(blocks, SPAN, N)
    out_coeff = conv_act[:, DI + N :].reshape(blocks, SPAN, N)
    step_size = jax.nn.softplus(step_raw + step_bias).reshape(blocks, SPAN, H)
    decays = -jnp.exp(log_rate) * step_size
    inside = jnp.cumsum(decays, axis=1)
    inside_heads = jnp.swapaxes(inside, 1, 2)
    step_heads = jnp.swapaxes(step_size, 1, 2)
    scores = jnp.einsum("ktn,ksn->kts", out_coeff, in_coeff, precision=highest)
    log_gaps = inside_heads[:, :, :, None] - inside_heads[:, :, None, :]
    causal = jnp.arange(SPAN)[:, None] >= jnp.arange(SPAN)[None, :]
    decay_mat = jnp.exp(jnp.where(causal[None, None], log_gaps, -jnp.inf))
    decay_mat = decay_mat * scores[:, None] * step_heads[:, :, None, :]
    inner_out = jnp.einsum("khts,kshp->kthp", decay_mat, head_input, precision=highest)
    last_log = inside[:, -1:, :]
    tail_weight = jnp.exp(last_log - inside) * step_size
    span_state = jnp.einsum(
        "ksh,kshp,ksn->khpn", tail_weight, head_input, in_coeff, precision=highest
    )
    totals = last_log[:, 0, :]

    def carry_step(carry_state, block_item):
        block_total, block_state = block_item
        return (jnp.exp(block_total)[:, None, None] * carry_state + block_state, carry_state)

    final_state, entering = lax.scan(
        carry_step, jnp.zeros((H, P_SIZE, N), jnp.float32), (totals, span_state)
    )
    cross_out = jnp.einsum(
        "kth,ktn,khpn->kthp", jnp.exp(inside), out_coeff, entering, precision=highest
    )
    offsets = jnp.cumsum(totals, axis=0) - totals
    cumulative = (inside + offsets[:, None, :]).reshape(tokens, H)
    ssm_zero = (inner_out + cross_out).reshape(tokens, H, P_SIZE)
    return (
        ssm_zero,
        cumulative,
        out_coeff.reshape(tokens, N),
        head_input.reshape(tokens, H, P_SIZE),
        final_state,
    )


def section_two(
    projected, ssm_zero, cumulative, out_coeff, head_input, state_in, skip_gain, gate_gain
):
    tokens = projected.shape[0]
    gate_part = projected[:, :DI]
    entering = jnp.einsum("tn,hpn->thp", out_coeff, state_in, precision=highest)
    ssm_full = (
        ssm_zero
        + jnp.exp(cumulative)[:, :, None] * entering
        + skip_gain[None, :, None] * head_input
    )
    gated = ssm_full.reshape(tokens, DI) * jax.nn.silu(gate_part)
    return rms_scale(gated, gate_gain)


def join_states(earlier, later):
    return (earlier[0] + later[0], jnp.exp(later[0])[:, None, None] * earlier[1] + later[1])


def join_grads(earlier, later):
    return (earlier[0] + later[0], later[1] + jnp.exp(later[0])[:, None, None] * earlier[1])


def on_device(
    inputs,
    cotangent,
    inproj,
    outproj,
    norm_gain,
    gate_gain,
    conv_weight,
    conv_bias,
    step_bias,
    log_rate,
    skip_gain,
):
    stream = inputs[0].astype(jnp.float32)
    tokens = stream.shape[0]
    rim_start = tokens - CONV + 1
    layer_index = 0
    inproj_full = lax.all_gather(inproj[layer_index], "fsdp", axis=0, tiled=True)
    outproj_full = lax.all_gather(outproj[layer_index], "fsdp", axis=0, tiled=True)
    normed_f, pull_norm = jax.vjp(rms_scale, stream, norm_gain[layer_index])
    normed = normed_f.astype(jnp.bfloat16)
    projected = jnp.dot(normed, inproj_full, preferred_element_type=jnp.float32)
    rim_rows = passed_along(projected[rim_start:, DI : DI + XBC], "seq", 1)
    first_out, pull_first = jax.vjp(
        section_one,
        projected,
        rim_rows,
        conv_weight[layer_index],
        conv_bias[layer_index],
        step_bias[layer_index],
        log_rate[layer_index],
    )
    ssm_zero, cumulative, out_coeff, head_input, final_state = first_out
    total_log = cumulative[tokens - 1]
    entering = prefix(
        (total_log, final_state),
        "seq",
        join_states,
        (jnp.zeros_like(total_log), jnp.zeros_like(final_state)),
    )
    state_in = entering[1]
    mixed_f, pull_second = jax.vjp(
        section_two,
        projected,
        ssm_zero,
        cumulative,
        out_coeff,
        head_input,
        state_in,
        skip_gain[layer_index],
        gate_gain[layer_index],
    )
    mixed_out = mixed_f.astype(jnp.bfloat16)
    stream = stream + jnp.dot(mixed_out, outproj_full, preferred_element_type=jnp.float32)
    stored = [
        (
            inproj_full,
            outproj_full,
            normed,
            mixed_out,
            pull_norm,
            pull_first,
            pull_second,
            total_log,
            state_in,
        )
    ]
    output = stream.astype(jnp.bfloat16)
    grad_stream = cotangent[0].astype(jnp.float32)
    inproj_list = [None] * LAYERS
    outproj_list = [None] * LAYERS
    small_list = [None] * LAYERS
    contract_rows = (((0,), (0,)), ((), ()))
    for layer_index in reversed(range(LAYERS)):
        (
            inproj_full,
            outproj_full,
            normed,
            mixed_out,
            pull_norm,
            pull_first,
            pull_second,
            total_log,
            state_in,
        ) = stored[layer_index]
        out_grad = grad_stream.astype(jnp.bfloat16)
        mix_grad = jnp.dot(out_grad, outproj_full.T, preferred_element_type=jnp.float32)
        second_grads = pull_second(mix_grad)
        (
            proj_second,
            zero_grad,
            cum_part,
            coeff_grad,
            head_grad,
            state_grad,
            skip_part,
            gate_part,
        ) = second_grads
        later = carried_in(
            (total_log, state_grad),
            "seq",
            join_grads,
            (jnp.zeros_like(total_log), jnp.zeros_like(state_grad)),
        )
        later_grad = later[1]
        total_grad = jnp.sum(later_grad * state_in, axis=(1, 2)) * jnp.exp(total_log)
        cum_grad = cum_part.at[tokens - 1].add(total_grad)
        first_grads = pull_first((zero_grad, cum_grad, coeff_grad, head_grad, later_grad))
        proj_first, rim_grad, kernel_part, bias_part, step_part, rate_part = first_grads
        rim_back = passed_along(rim_grad, "seq", -1)
        proj_grad = (proj_first + proj_second).at[rim_start:, DI : DI + XBC].add(rim_back)
        proj_grad_b = proj_grad.astype(jnp.bfloat16)
        normed_grad = jnp.dot(proj_grad_b, inproj_full.T, preferred_element_type=jnp.float32)
        stream_part, norm_part = pull_norm(normed_grad)
        grad_stream = grad_stream + stream_part
        inproj_term = lax.dot_general(
            normed, proj_grad_b, contract_rows, preferred_element_type=jnp.float32
        )
        outproj_term = lax.dot_general(
            mixed_out, out_grad, contract_rows, preferred_element_type=jnp.float32
        )
        inproj_owned, outproj_owned = (
            lax.psum_scatter(
                inproj_term.astype(jnp.bfloat16), "fsdp", scatter_dimension=0, tiled=True
            ).astype(jnp.float32),
            lax.psum_scatter(
                outproj_term.astype(jnp.bfloat16), "fsdp", scatter_dimension=0, tiled=True
            ).astype(jnp.float32),
        )
        inproj_sum, outproj_sum = lax.psum((inproj_owned, outproj_owned), "seq")
        inproj_list[layer_index] = inproj_sum
        outproj_list[layer_index] = outproj_sum
        small_list[layer_index] = (
            norm_part,
            gate_part,
            kernel_part,
            bias_part,
            step_part,
            rate_part,
            skip_part,
        )
    norm_all, gate_all, kernel_all, bias_all, step_all, rate_all, skip_all = [
        jnp.stack([entry[member] for entry in small_list]) for member in range(7)
    ]
    norm_grad, gate_grad, kernel_grad, bias_grad, step_grad, rate_grad, skip_grad = lax.psum(
        (norm_all, gate_all, kernel_all, bias_all, step_all, rate_all, skip_all), ("seq", "fsdp")
    )
    return (
        output[None],
        grad_stream.astype(jnp.bfloat16)[None],
        jnp.stack(inproj_list),
        jnp.stack(outproj_list),
        norm_grad,
        gate_grad,
        kernel_grad,
        bias_grad,
        step_grad,
        rate_grad,
        skip_grad,
    )


def solution(mesh):
    placed = (
        P("fsdp", "seq", None),
        P("fsdp", "seq", None),
        P(None, "fsdp", None),
        P(None, "fsdp", None),
        P(),
        P(),
        P(),
        P(),
        P(),
        P(),
        P(),
    )
    return jax.shard_map(
        on_device,
        mesh=mesh,
        in_specs=placed,
        out_specs=(
            P("fsdp", "seq", None),
            P("fsdp", "seq", None),
            P(None, "fsdp", None),
            P(None, "fsdp", None),
            P(),
            P(),
            P(),
            P(),
            P(),
            P(),
            P(),
        ),
        check_vma=False,
    )
```

profile of v0, /device:TPU:0, one launch (start us, length us, event | category | flops | bytes accessed | tf_op | source)
XLA Modules:
  0.0 551.0 jit_solution(2837934593614807210)
XLA Ops:
  12.7 40.4 %all-gather.10.cloned.1.call-done = bf16[1,768,3352]{2,1,0:T(8,128)(2,1)} async-done(((bf16[1,192,3352]{2,1,0:T(8,128)(2,1)}), bf16[1,768,3352]{2,1,0:T(8,128)(2,1)}) %all-gather.10.cloned.1.call-update) | async-done | bytes 5148688 | tf_op jit(solution)/shard_map/all_gather | solution.py:170
  53.1 4.7 fusion.8
  61.1 3.5 collective-permute-start
  67.7 5.5 fusion.74
  74.8 2.0 reshape.345
  76.8 2.5 copy.376
  79.3 5.0 fusion.37
  84.5 4.3 while.68
  99.8 22.0 %all-gather.4 = bf16[8,1,24]{2,1,0:T(2,128)(2,1)S(1)} all-gather(bf16[1,1,24]{2,1,0:T(2,128)(2,1)} %bitcast.264), channel_id=1, replica_groups=mesh['seq'=8,'fsdp'=4] {'seq'}, dimensions={0}, use_global_device_ids=true | all-gather | bytes 432 | tf_op jit(solution)/shard_map/all_gather | solution.py:29
  125.1 2.4 fusion.141
  127.6 3.2 fusion.22
  132.0 1.8 reshape.349
  133.7 16.8 %all-gather.12.cloned.1.call-done = bf16[192,64,128]{2,1,0:T(8,128)(2,1)} async-done(((bf16[24,64,128]{2,1,0:T(8,128)(2,1)}), bf16[192,64,128]{2,1,0:T(8,128)(2,1)}) %all-gather.12.cloned.1.call-update) | async-done | bytes 3145744 | tf_op jit(solution)/shard_map/all_gather | solution.py:29
  150.6 15.3 %while.69 = (s32[]{:T(128)}, f32[24,64,128]{2,1,0:T(8,128)S(1)}, s32[]{:T(128)}, bf16[8,24]{1,0:T(8,128)(2,1)}, bf16[8,24,64,128]{3,2,1,0:T(8,128)(2,1)}, /*index=5*/s32[]{:T(128)}, s32[]{:T(128)}) while((s32[]{:T(128)}, f32[24,64,128]{2,1,0:T(8,128)S(1)}, s32[]{:T(128)}, bf16[8,24]{1,0:T(8,128)(2,1)}, ...), condition=%wide.region_6.7_spmd.clone, body=%wide.region_5.6_spmd.clone.sunk | while | flops 983068 | bytes 1966433 | solution.py:46
  170.3 4.6 all-gather.14.cloned.1.call-done
  174.9 3.3 multiply_reduce_fusion.8
  178.3 2.2 multiply_reduce_fusion.7
  183.3 2.2 reshape.353
  185.5 2.1 copy.399
  187.6 3.4 fusion.59
  191.1 2.8 fusion.65
  193.9 4.2 fusion.69
  202.6 2.8 fusion.20
  205.4 2.2 convolution_convert_fusion.1
  207.9 35.3 %all-gather.16.cloned.1.call-done = bf16[192,64,128]{2,1,0:T(8,128)(2,1)} async-done(((bf16[24,64,128]{2,1,0:T(8,128)(2,1)}), bf16[192,64,128]{2,1,0:T(8,128)(2,1)}) %all-gather.16.cloned.1.call-update) | async-done | bytes 3145744 | tf_op jit(solution)/shard_map/all_gather | solution.py:52
  243.2 15.4 %while.70 = (s32[]{:T(128)}, f32[24,64,128]{2,1,0:T(8,128)S(1)}, s32[]{:T(128)}, bf16[8,24,64,128]{3,2,1,0:T(8,128)(2,1)}, bf16[8,24]{1,0:T(8,128)(2,1)}, /*index=5*/s32[]{:T(128)}, s32[]{:T(128)}, s32[]{:T(128)}, s32[]{:T(128)}) while((s32[]{:T(128)}, f32[24,64,128]{2,1,0:T(8,128)S(1)}, s32[]{:T(128)}, ...), condition=%wide.region_10.11_spmd.clone, body=%wide.region_9.10_spmd.clone.sunk | while | flops 983072 | bytes 1966495 | solution.py:70
  262.0 6.6 %while.67 = (s32[]{:T(128)}, f32[24,64,128]{2,1,0:T(8,128)S(1)}, f32[2,24]{1,0:T(2,128)S(1)}, f32[2,24,64,128]{3,2,1,0:T(8,128)}, f32[2,24,64,128]{3,2,1,0:T(8,1...) while((s32[]{:T(128)}, f32[24,64,128]{2,1,0:T(8,128)S(1)}, ...), condition=%wide.region_13.14_spmd, body=%wide.region_11.13_spmd.sunk | while | flops 786435 | bytes 11011073 | solution.py:112
  269.2 3.9 fusion.56
  273.2 4.6 fusion.142
  277.9 4.8 bitcast_add_fusion.2
  283.6 3.8 copy.420
  287.4 2.1 copy.406
  289.5 2.5 reshape.358
  293.5 6.2 %multiply_reduce_fusion.5 = (f32[1792]{0:T(1024)}, f32[1792]{0:T(1024)}, f32[1792]{0:T(1024)}, f32[1792]{0:T(1024)}, f32[1792]{0:T(1024)}, /*index=5*/f32[128,1792]{0,1:T(8,128)S(1)}) fusion(f32[128,1792]{0,1:T(8,128)} %slice.113, f32[3,1792]{0,1:T(8,128)} %copy.364, f32[128,3352]{0,1:T(8,128)S(1)} %copy-done.10, f32[128,1792]{0,1:T(8,128)} %get-tuple-element.620, ...), kind=kLoop, calls=%fused_computation.93 | loop fusion | flops 5266688 | bytes 4644864 | tf_op jit(solution)/shard_map/transpose(jvp())/reduce_sum | solution.py:84
  305.8 3.1 multiply_reduce_fusion
  310.9 2.1 copy.407
  316.3 2.7 collective-permute-done.1
  319.1 2.0 copy.408
  322.6 8.7 %scatter-add.9 = f32[128,3352]{0,1:T(8,128)S(1)} dynamic-update-slice(f32[128,3352]{0,1:T(8,128)S(1)} %pad_add_fusion.1, f32[3,1792]{0,1:T(8,128)S(1)} %slice_add_fusion, s32[]{:T(128)} %constant.233.clone.1, s32[]{:T(128)} %constant.234.clone.1) | dynamic-update-slice | bytes 43012 | tf_op jit(solution)/shard_map/scatter-add | solution.py:263
  331.3 4.0 convolution_convert_fusion
  335.4 2.2 bitcast_convert_fusion.1
  337.6 49.3 %reduce-scatter.3.cloned.1.call-done = bf16[192,3352]{1,0:T(8,128)(2,1)} async-done(((bf16[768,3352]{1,0:T(8,128)(2,1)}), bf16[192,3352]{1,0:T(8,128)(2,1)}) %reduce-scatter.3.cloned.1.call-update) | async-done | bytes 1287184 | tf_op jit(solution)/shard_map/reduce_scatter | solution.py:275
  386.9 3.0 bitcast_convert_fusion
  391.1 3.1 fusion.53
  394.5 4.8 fusion.102
  399.3 44.4 %all-reduce.15 = (f32[1,768]{1,0:T(1,128)}, f32[1,1536]{1,0:T(1,128)}, f32[1,4,1792]{2,1,0:T(4,128)}, f32[1,1792]{1,0:T(1,128)}, f32[1,24]{1,0:T(1,128)}, /*index=5*/f32[1,24]{1,0:T(1,128)}, f32[1,24]{1,0:T(1,128)}) all-reduce(f32[1,768]{1,0:T(1,128)S(1)} %reshape.359, ...), channel_id=1, replica_groups=mesh['seq'=8,'fsdp'=4] {'seq','fsdp'}, use_global_device_ids=true, to_apply=%region_30.31 | all-reduce | flops 11336 | bytes 90688 | tf_op jit(solution)/shard_map/psum | solution.py:297
  444.6 94.6 %all-reduce.19.cloned.1.call-done = (f32[1,192,3352]{2,1,0:T(8,128)}, f32[1,384,768]{2,1,0:T(8,128)}) async-done(((f32[1,192,3352]{2,1,0:T(8,128)}, f32[1,384,768]{2,1,0:T(8,128)}), (f32[1,192,3352]{2,1,0:T(8,128)}, f32[1,384,768]{2,1,0:T(8,128)})) %all-reduce.19.cloned.1.call-update) | async-done | bytes 3754000 | tf_op jit(solution)/shard_map/psum | solution.py:282
  539.2 3.5 copy.534
  (400 shorter events, 104.4 us)
Async XLA Ops:
  7.2 45.9 %copy-start.21 = (bf16[1,128,768]{2,1,0:T(8,128)(2,1)S(1)}, bf16[1,128,768]{2,1,0:T(8,128)(2,1)}, u32[]{:S(2)}) copy-start(bf16[1,128,768]{2,1,0:T(8,128)(2,1)} %param.23) | copy-start | bytes 589828
  7.2 5.5 copy-start.113
  7.2 45.9 %all-gather.10.cloned.1.call-start = ((), (), s32[]{:S(2)}) async-start(), calls=%async_computation.4 | async-start | bytes 6635520 | tf_op jit(solution)/shard_map/all_gather | solution.py:170
  7.9 142.6 %all-gather.12.cloned.1.call-start = ((), (), s32[]{:S(2)}) async-start(), calls=%async_computation.5 | async-start | bytes 3538944 | tf_op jit(solution)/shard_map/all_gather | solution.py:29
  11.6 56.0 %copy-start.67 = (f32[1792]{0:T(1024)}, f32[1792]{0:T(1024)S(1)}, u32[]{:S(2)}) copy-start(f32[1792]{0:T(1024)S(1)} %get-tuple-element.543) | copy-start | bytes 21508
  12.7 45.1 %copy-start.107 = (f32[128]{0:T(128)}, f32[128]{0:T(128)S(1)}, u32[]{:S(2)}) copy-start(f32[128]{0:T(128)S(1)} %fusion.105) | copy-start | bytes 1540
  12.7 45.3 %copy-start.98 = (f32[24]{0:T(128)}, f32[24]{0:T(128)S(1)}, u32[]{:S(2)}) copy-start(f32[24]{0:T(128)S(1)} %negate_bitcast_fusion) | copy-start | bytes 292
  12.7 45.1 %copy-start.91 = (f32[128]{0:T(128)}, f32[128]{0:T(128)S(1)}, u32[]{:S(2)}) copy-start(f32[128]{0:T(128)S(1)} %fusion.124) | copy-start | bytes 1540
  12.7 45.1 %copy-start.101 = (f32[1,24]{1,0:T(1,128)S(1)}, f32[1,24]{1,0:T(1,128)}, u32[]{:S(2)}) copy-start(f32[1,24]{1,0:T(1,128)} %param.31) | copy-start | bytes 292
  57.8 7.5 %copy-start.8 = (f32[128,3352]{0,1:T(8,128)}, f32[128,3352]{0,1:T(8,128)S(1)}, u32[]{:S(2)}) copy-start(f32[128,3352]{0,1:T(8,128)S(1)} %fusion.8) | copy-start | bytes 5148676
  58.0 6.6 %copy-start.40 = (f32[2,64,24]{1,0,2:T(2,128)}, f32[2,64,24]{1,0,2:T(2,128)S(1)}, u32[]{:S(2)}) copy-start(f32[2,64,24]{1,0,2:T(2,128)S(1)} %reshape.346) | copy-start | bytes 36868
  58.3 8.0 %copy-start.37 = (f32[2,64,24]{2,1,0:T(8,128)}, f32[2,64,24]{2,1,0:T(8,128)S(1)}, u32[]{:S(2)}) copy-start(f32[2,64,24]{2,1,0:T(8,128)S(1)} %reduce_window_sum.46) | copy-start | bytes 36868
  58.4 7.9 %copy-start.42 = (f32[2,64,24]{1,2,0:T(8,128)}, f32[2,64,24]{1,2,0:T(8,128)S(1)}, u32[]{:S(2)}) copy-start(f32[2,64,24]{1,2,0:T(8,128)S(1)} %copy.373) | copy-start | bytes 36868
  61.1 6.5 %copy-start.69 = (f32[1792]{0:T(1024)S(1)}, f32[1792]{0:T(1024)}, u32[]{:S(2)}) copy-start(f32[1792]{0:T(1024)} %get-tuple-element.544) | copy-start | bytes 21508
  61.1 6.5 %copy-start.71 = (f32[1792]{0:T(1024)S(1)}, f32[1792]{0:T(1024)}, u32[]{:S(2)}) copy-start(f32[1792]{0:T(1024)} %get-tuple-element.545) | copy-start | bytes 21508
  61.1 6.5 %copy-start.73 = (f32[1792]{0:T(1024)S(1)}, f32[1792]{0:T(1024)}, u32[]{:S(2)}) copy-start(f32[1792]{0:T(1024)} %get-tuple-element.546) | copy-start | bytes 21508
  61.1 6.5 %copy-start.87 = (f32[1792]{0:T(1024)S(1)}, f32[1792]{0:T(1024)}, u32[]{:S(2)}) copy-start(f32[1792]{0:T(1024)} %reduce.9) | copy-start | bytes 21508
  61.1 5.2 collective-permute-start
  73.1 92.8 %copy-start.22 = (f32[128,1792]{0,1:T(8,128)}, f32[128,1792]{0,1:T(8,128)S(1)}, u32[]{:S(2)}) copy-start(f32[128,1792]{0,1:T(8,128)S(1)} %get-tuple-element.619) | copy-start | bytes 2752516
  79.3 5.0 copy-start.5
  88.8 6.0 %copy-start.78 = (f32[2,24]{1,0:T(2,128)}, f32[2,24]{1,0:T(2,128)S(1)}, u32[]{:S(2)}) copy-start(f32[2,24]{1,0:T(2,128)S(1)} %get-tuple-element.947) | copy-start | bytes 580
  88.8 6.0 %copy-start.96 = (f32[2,24]{1,0:T(2,128)}, f32[2,24]{1,0:T(2,128)S(1)}, u32[]{:S(2)}) copy-start(f32[2,24]{1,0:T(2,128)S(1)} %get-tuple-element.879) | copy-start | bytes 580
  88.8 38.7 %copy-start = (f32[2,24,64,128]{3,2,1,0:T(8,128)}, f32[2,24,64,128]{3,2,1,0:T(8,128)S(1)}, u32[]{:S(2)}) copy-start(f32[2,24,64,128]{3,2,1,0:T(8,128)S(1)} %get-tuple-element.878) | copy-start | bytes 4718596
  89.7 85.2 %all-gather.14.cloned.1.call-start = ((), (), s32[]{:S(2)}) async-start(), calls=%async_computation.6 | async-start | bytes 2949120 | tf_op jit(solution)/shard_map/all_gather | solution.py:171
  90.5 152.8 %all-gather.16.cloned.1.call-start = ((), (), s32[]{:S(2)}) async-start(), calls=%async_computation.7 | async-start | bytes 3538944 | tf_op jit(solution)/shard_map/all_gather | solution.py:52
  95.6 31.8 %copy-start.54 = (f32[128,24]{0,1:T(8,128)}, f32[128,24]{0,1:T(8,128)S(1)}, u32[]{:S(2)}) copy-start(f32[128,24]{0,1:T(8,128)S(1)} %copy.379) | copy-start | bytes 36868
  169.3 8.9 %copy-start.11 = (f32[128,1536]{0,1:T(8,128)}, f32[128,1536]{0,1:T(8,128)S(1)}, u32[]{:S(2)}) copy-start(f32[128,1536]{0,1:T(8,128)S(1)} %get-tuple-element.618) | copy-start | bytes 2359300
  183.0 152.4 %reduce-scatter.5.cloned.1.call-start = ((), (), s32[]{:S(2)}) async-start(), calls=%async_computation.3 | async-start | bytes 2949120 | tf_op jit(solution)/shard_map/reduce_scatter | solution.py:278
  207.7 179.2 %reduce-scatter.3.cloned.1.call-start = ((), (), s32[]{:S(2)}) async-start(), calls=%async_computation.2 | async-start | bytes 6635520 | tf_op jit(solution)/shard_map/reduce_scatter | solution.py:275
  262.0 7.2 %copy-start.47 = (f32[2,64,24]{1,2,0:T(8,128)S(1)}, f32[2,64,24]{1,2,0:T(8,128)}, u32[]{:S(2)}) copy-start(f32[2,64,24]{1,2,0:T(8,128)} %get-tuple-element.631) | copy-start | bytes 36868
  273.1 4.7 copy-start.15
  273.2 4.7 copy-start.46
  277.9 4.8 copy-start.18
  277.9 4.8 copy-start.53
  293.5 6.3 %copy-start.68 = (f32[1792]{0:T(1024)S(1)}, f32[1792]{0:T(1024)}, u32[]{:S(2)}) copy-start(f32[1792]{0:T(1024)} %copy-done.67) | copy-start | bytes 21508
  293.5 6.3 %copy-start.70 = (f32[1792]{0:T(1024)S(1)}, f32[1792]{0:T(1024)}, u32[]{:S(2)}) copy-start(f32[1792]{0:T(1024)} %get-tuple-element.544) | copy-start | bytes 21508
  293.5 6.3 %copy-start.72 = (f32[1792]{0:T(1024)S(1)}, f32[1792]{0:T(1024)}, u32[]{:S(2)}) copy-start(f32[1792]{0:T(1024)} %get-tuple-element.545) | copy-start | bytes 21508
  293.5 6.3 %copy-start.74 = (f32[1792]{0:T(1024)S(1)}, f32[1792]{0:T(1024)}, u32[]{:S(2)}) copy-start(f32[1792]{0:T(1024)} %get-tuple-element.546) | copy-start | bytes 21508
  305.8 4.9 copy-start.90
  305.8 4.9 copy-start.99
  308.9 5.4 copy-start.102
  308.9 6.1 %copy-start.31 = (f32[128,1536]{0,1:T(8,128)S(1)}, f32[128,1536]{0,1:T(8,128)}, u32[]{:S(2)}) copy-start(f32[128,1536]{0,1:T(8,128)} %get-tuple-element.623) | copy-start | bytes 2359300
  313.0 6.1 %collective-permute-start.1 = (f32[3,1792]{1,0:T(4,128)}, f32[3,1792]{1,0:T(4,128)}, u32[]{:S(2)}, u32[]{:S(2)}) collective-permute-start(f32[3,1792]{1,0:T(4,128)} %copy.407), channel_id=1, source_target_pairs={{4,0},{8,4},{12,8},{16,12},{20,16},{24,20},{28,24},{5,1},{9,5},{13... | collective-permute-start | bytes 64520 | tf_op jit(solution)/shard_map/ppermute | solution.py:23
  322.6 8.7 %copy-start.92 = (f32[128]{0:T(128)S(1)}, f32[128]{0:T(128)}, u32[]{:S(2)}) copy-start(f32[128]{0:T(128)} %copy-done.91) | copy-start | bytes 1540
  335.3 203.8 %all-reduce.19.cloned.1.call-start = ((), (), s32[]{:S(2)}) async-start(), calls=%async_computation.8 | async-start | bytes 7667712 | tf_op jit(solution)/shard_map/psum | solution.py:282
  394.5 4.8 copy-start.100
  394.5 49.2 %copy-start.108 = (f32[128]{0:T(128)S(1)}, f32[128]{0:T(128)}, u32[]{:S(2)}) copy-start(f32[128]{0:T(128)} %copy-done.107) | copy-start | bytes 1540
  394.5 49.2 %copy-start.34 = (bf16[1,128,768]{2,1,0:T(8,128)(2,1)S(1)}, bf16[1,128,768]{2,1,0:T(8,128)(2,1)}, u32[]{:S(2)}) copy-start(bf16[1,128,768]{2,1,0:T(8,128)(2,1)} %param.24) | copy-start | bytes 589828
  (78 other events, 196.5 us)
Sparse Core Ops, SparseCore 0:
  9.6 43.4 all-gather.9
  89.8 60.6 all-gather.11
  152.1 22.6 all-gather.13
  183.1 60.0 all-gather.15
  246.2 31.4 reduce-scatter.4
  335.5 51.4 reduce-scatter.2
  391.2 147.9 all-reduce.18
where the time goes:
time: 561 us; the launch traced here: 551 us
  waiting for transfers between devices  245 us (44%)
  other arithmetic  78.3 us (14%)
  local copies, waits for them, and re-layouts  75.6 us (13%)
  blocking collectives  66.4 us (12%)
  matrix products  63.5 us (11%)
  between operations  16 us (3%)
    psum x1, waiting for transfers between devices, on_device(): inproj_sum, outproj_sum = lax.psum((inproj_owned, outproj_owned), 'seq')  94.6 us
    reduce_scatter x1, waiting for transfers between devices, on_device(): lax.psum_scatter(inproj_term.astype(jnp.bfloat16), 'fsdp', scatter_dimens...  49.3 us
    psum x1, blocking collectives, on_device(): lax.psum((norm_all, gate_all, kernel_all, bias_all, step_all, rate_all, s...  44.4 us
    all_gather x1, waiting for transfers between devices, on_device(): lax.all_gather(inproj[layer_index], 'fsdp', axis=0, tiled=True)  40.4 us
    all_gather x1, waiting for transfers between devices, carried_in(): lax.all_gather(part.astype(kind), axis)  35.3 us
    all_gather x1, blocking collectives, prefix(): lax.all_gather(part.astype(kind), axis)  22 us
    unnamed x231, local copies, waits for them, and re-layouts  17.7 us
    all_gather x1, waiting for transfers between devices, prefix(): lax.all_gather(part.astype(kind), axis)  16.8 us
  transfers between devices with their start and end apart: 9, of which 7 were waited for; matrix products, arithmetic and copies ran while one was open for 30% of the time, Pallas kernels for 0%

commit v1 on v0

v1 whole, which is shorter than its diff:
```python
import jax
import jax.numpy as jnp
from jax import lax
from jax.sharding import PartitionSpec as P

H = 24
P_SIZE = 64
N = 128
CONV = 4
SPAN = 64
LAYERS = 1
DI = 1536
XBC = 1792


epsilon = 1e-05
highest = lax.Precision.HIGHEST


def passed_along(shard, axis, by):
    length = lax.axis_size(axis)
    pairs = [(i, i + by) for i in range(length) if 0 <= i + by < length]
    return lax.ppermute(shard, axis, pairs)


def span_weights(totals, index, forward):
    length = totals.shape[0]
    source = jnp.arange(length)[:, None]
    middle = jnp.arange(length)[None, :]
    if forward:
        between = (middle > source) & (middle < index)
        reached = jnp.arange(length) < index
    else:
        between = (middle < source) & (middle > index)
        reached = jnp.arange(length) > index
    logs = jnp.sum(jnp.where(between[:, :, None], totals[None], 0.0), axis=1)
    return jnp.where(reached[:, None], jnp.exp(logs), 0.0)


def weighted(parts, weights):
    return jnp.sum(weights[:, :, None, None] * parts.astype(jnp.float32), axis=0)


def rms_scale(values, gain):
    return values * lax.rsqrt(jnp.mean(values * values, axis=-1, keepdims=True) + epsilon) * gain


def section_one(projected, rim_rows, conv_weight, conv_bias, step_bias, log_rate):
    tokens = projected.shape[0]
    conv_input = projected[:, DI : DI + XBC]
    step_raw = projected[:, DI + XBC :]
    extended = jnp.concatenate([rim_rows, conv_input], axis=0)
    conv_sum = conv_bias + conv_weight[0] * extended[0:tokens]
    for offset in range(1, CONV):
        conv_sum = conv_sum + conv_weight[offset] * extended[offset : offset + tokens]
    conv_act = jax.nn.silu(conv_sum)
    blocks = 1
    head_input = conv_act[:, :DI].reshape(blocks, tokens, H, P_SIZE)
    in_coeff = conv_act[:, DI : DI + N].reshape(blocks, tokens, N)
    out_coeff = conv_act[:, DI + N :].reshape(blocks, tokens, N)
    step_size = jax.nn.softplus(step_raw + step_bias).reshape(blocks, tokens, H)
    decays = -jnp.exp(log_rate) * step_size
    inside = jnp.cumsum(decays, axis=1)
    inside_heads = jnp.swapaxes(inside, 1, 2)
    step_heads = jnp.swapaxes(step_size, 1, 2)
    scores = jnp.einsum("ktn,ksn->kts", out_coeff, in_coeff, precision=highest)
    log_gaps = inside_heads[:, :, :, None] - inside_heads[:, :, None, :]
    causal = jnp.arange(tokens)[:, None] >= jnp.arange(tokens)[None, :]
    decay_mat = jnp.exp(jnp.where(causal[None, None], log_gaps, -jnp.inf))
    decay_mat = decay_mat * scores[:, None] * step_heads[:, :, None, :]
    inner_out = jnp.einsum("khts,kshp->kthp", decay_mat, head_input, precision=highest)
    last_log = inside[:, -1:, :]
    tail_weight = jnp.exp(last_log - inside) * step_size
    span_state = jnp.einsum(
        "ksh,kshp,ksn->khpn", tail_weight, head_input, in_coeff, precision=highest
    )

    final_state = span_state[0]
    cumulative = inside.reshape(tokens, H)
    ssm_zero = inner_out.reshape(tokens, H, P_SIZE)
    return (
        ssm_zero,
        cumulative,
        out_coeff.reshape(tokens, N),
        head_input.reshape(tokens, H, P_SIZE),
        final_state,
    )


def section_two(
    projected, ssm_zero, cumulative, out_coeff, head_input, state_in, skip_gain, gate_gain
):
    tokens = projected.shape[0]
    gate_part = projected[:, :DI]
    entering = jnp.einsum("tn,hpn->thp", out_coeff, state_in, precision=highest)
    ssm_full = (
        ssm_zero
        + jnp.exp(cumulative)[:, :, None] * entering
        + skip_gain[None, :, None] * head_input
    )
    gated = ssm_full.reshape(tokens, DI) * jax.nn.silu(gate_part)
    return rms_scale(gated, gate_gain)


def on_device(
    inputs,
    cotangent,
    inproj,
    outproj,
    norm_gain,
    gate_gain,
    conv_weight,
    conv_bias,
    step_bias,
    log_rate,
    skip_gain,
):
    stream = inputs[0].astype(jnp.float32)
    tokens = stream.shape[0]
    rim = CONV - 1
    rim_start = tokens - rim
    index, shard = lax.axis_index("seq"), lax.axis_index("fsdp")
    inproj_full = lax.all_gather(inproj[0], "fsdp", axis=0, tiled=True)
    halo = passed_along(inputs[0, rim_start:], "seq", 1).astype(jnp.float32)
    normed_f, pull_norm = jax.vjp(rms_scale, stream, norm_gain[0])
    normed = normed_f.astype(jnp.bfloat16)
    halo_normed = rms_scale(halo, norm_gain[0]).astype(jnp.bfloat16)
    extra = jnp.pad(halo_normed, ((0, 8 - rim), (0, 0)))
    both = jnp.dot(
        jnp.concatenate([normed, extra], axis=0), inproj_full, preferred_element_type=jnp.float32
    )
    projected = both[:tokens]
    rim_rows = both[tokens : tokens + rim, DI : DI + XBC]
    outproj_full = lax.all_gather(outproj[0], "fsdp", axis=0, tiled=True)
    first_out, pull_first = jax.vjp(
        section_one, projected, rim_rows, conv_weight[0], conv_bias[0], step_bias[0], log_rate[0]
    )
    ssm_zero, cumulative, out_coeff, head_input, final_state = first_out
    total_log = cumulative[tokens - 1]
    totals = lax.all_gather(total_log, "seq")
    states = lax.all_gather(final_state.astype(jnp.bfloat16), "seq")
    state_in = weighted(states, span_weights(totals, index, True))
    mixed_f, pull_second = jax.vjp(
        section_two,
        projected,
        ssm_zero,
        cumulative,
        out_coeff,
        head_input,
        state_in,
        skip_gain[0],
        gate_gain[0],
    )
    mixed_out = mixed_f.astype(jnp.bfloat16)
    output = stream + jnp.dot(mixed_out, outproj_full, preferred_element_type=jnp.float32)
    out_grad = cotangent[0]
    mix_grad = jnp.dot(out_grad, outproj_full.T, preferred_element_type=jnp.float32)
    (
        proj_second,
        zero_grad,
        cum_part,
        coeff_grad,
        head_grad,
        state_grad,
        skip_part,
        gate_part,
    ) = pull_second(mix_grad)
    state_grads = lax.all_gather(state_grad.astype(jnp.bfloat16), "seq")
    later_grad = weighted(state_grads, span_weights(totals, index, False))
    total_grad = jnp.sum(later_grad * state_in, axis=(1, 2)) * jnp.exp(total_log)
    cum_grad = cum_part + jnp.pad(total_grad[None], ((tokens - 1, 0), (0, 0)))
    proj_first, rim_grad, kernel_part, bias_part, step_part, rate_part = pull_first(
        (zero_grad, cum_grad, coeff_grad, head_grad, later_grad)
    )
    rim_back = passed_along(rim_grad, "seq", -1)
    proj_grad = (
        proj_first
        + proj_second
        + jnp.pad(rim_back, ((rim_start, 0), (DI, projected.shape[1] - DI - XBC)))
    )
    proj_grad_b = proj_grad.astype(jnp.bfloat16)
    return finish(
        inputs, cotangent, inproj, outproj, stream, pull_norm, normed, mixed_out, output,
        inproj_full, proj_grad_b, shard,
        (gate_part, kernel_part, bias_part, step_part, rate_part, skip_part),
    )


def finish(
    inputs, cotangent, inproj, outproj, stream, pull_norm, normed, mixed_out, output,
    inproj_full, proj_grad_b, shard, parts,
):
    in_rows, out_rows = inproj.shape[1], outproj.shape[1]
    width = proj_grad_b.shape[1]
    grads_all = lax.all_gather(proj_grad_b, "fsdp")
    normed_all = lax.all_gather(normed.T, "fsdp")
    mixed_all = lax.all_gather(mixed_out.T, "fsdp")
    outer_all = lax.all_gather(cotangent[0], "fsdp")
    normed_own = lax.dynamic_slice_in_dim(normed_all, shard * in_rows, in_rows, 1)
    mixed_own = lax.dynamic_slice_in_dim(mixed_all, shard * out_rows, out_rows, 1)
    outproj_term = jnp.einsum("fkt,ftc->kc", mixed_own, outer_all, preferred_element_type=jnp.float32)
    normed_grad = jnp.dot(proj_grad_b, inproj_full.T, preferred_element_type=jnp.float32)
    stream_part, norm_part = pull_norm(normed_grad)
    grad_stream = cotangent[0].astype(jnp.float32) + stream_part
    small = [norm_part] + list(parts)
    sizes = [part.size for part in small]
    total = sum(sizes)
    rows = -(-total // width)
    lines = -(-total // 1024) * 8
    flat = jnp.concatenate([part.reshape(-1) for part in small] + [jnp.zeros((lines * 128 - total,), jnp.float32)])
    group = jnp.sum(lax.all_gather(flat.reshape(lines, 128), "fsdp"), axis=0).reshape(-1)
    group = jnp.pad(group[:total], (0, rows * width - total)).reshape(rows, width)
    inproj_term = jnp.einsum("fkt,ftc->kc", normed_own, grads_all, preferred_element_type=jnp.float32)
    joined = jnp.concatenate([inproj_term, group], axis=0).astype(jnp.bfloat16)
    joined_sum, outproj_sum = lax.psum((joined, outproj_term.astype(jnp.bfloat16)), "seq")
    inproj_grad = joined_sum[:in_rows].astype(jnp.float32)
    flat = joined_sum[in_rows:].astype(jnp.float32).reshape(-1)
    outs, at = [], 0
    for part, size in zip(small, sizes):
        outs.append(flat[at : at + size].reshape((1,) + part.shape))
        at += size
    return (
        output.astype(jnp.bfloat16)[None],
        grad_stream.astype(jnp.bfloat16)[None],
        inproj_grad[None],
        outproj_sum.astype(jnp.float32)[None],
        *outs,
    )


def solution(mesh):
    placed = (
        P("fsdp", "seq", None),
        P("fsdp", "seq", None),
        P(None, "fsdp", None),
        P(None, "fsdp", None),
        P(),
        P(),
        P(),
        P(),
        P(),
        P(),
        P(),
    )
    return jax.shard_map(
        on_device,
        mesh=mesh,
        in_specs=placed,
        out_specs=(
            P("fsdp", "seq", None),
            P("fsdp", "seq", None),
            P(None, "fsdp", None),
            P(None, "fsdp", None),
            P(),
            P(),
            P(),
            P(),
            P(),
            P(),
            P(),
        ),
        check_vma=False,
    )
```

time: 561 us -> 411 us (0.73); the launches traced: 551 us -> 410 us
  local copies, waits for them, and re-layouts: 75.6 us -> 17.2 us
  other arithmetic: 78.3 us -> 47.5 us
  matrix products: 63.5 us -> 43 us
  blocking collectives: 66.4 us -> 48.7 us
  waiting for transfers between devices: 245 us -> 231 us
    reduce_scatter x2 -> x0, waiting for transfers between devices: 49.4 us -> none  [the longest x1 49.3 us: on_device(): lax.psum_scatter(inproj_term.astype(jnp.bfloat16), 'fsdp', scatter_dimens...]
    psum x1 -> x0, blocking collectives: 44.4 us -> none  [on_device(): lax.psum((norm_all, gate_all, kernel_all, bias_all, step_all, rate_all, s...]
    all_gather x4 -> x6, waiting for transfers between devices: 97.1 us -> 134 us  [the longest x1 51.3 us: on_device(): state_grads = lax.all_gather(state_grad.astype(jnp.bfloat16), 'seq')]
    all_gather x1 -> x4, blocking collectives: 22 us -> 48.7 us  [the longest x1 21 us: on_device(): totals = lax.all_gather(total_log, 'seq')]
    select_n x17 -> x2, other arithmetic: 19.2 us -> 1.38 us  [span_weights(): return jnp.where(reached[:, None], jnp.exp(logs), 0.0)]
    unnamed x231 -> x128, local copies, waits for them, and re-layouts: 17.7 us -> 2.27 us
    exp x18 -> x0, other arithmetic: 13.3 us -> none  [the longest x8 5.56 us: join_states(): jnp.exp(later[0])[:, None, None] * earlier[1] + later[1]]
    reshape x13 -> x9, local copies, waits for them, and re-layouts: 15.6 us -> 3.3 us  [the longest x5 2.99 us: finish(): outs.append(flat[at:at + size].reshape((1,) + part.shape))]
  transfers between devices with their start and end apart: 9 -> 9, of which waited for: 7 -> 5; matrix products, arithmetic and copies ran while one was open for 30% -> 16% of each run, Pallas kernels for 0% -> 0%
where the time goes in v1:
time: 411 us; the launch traced here: 410 us
  waiting for transfers between devices  231 us (56%)
  blocking collectives  48.7 us (12%)
  other arithmetic  47.5 us (12%)
  matrix products  43 us (10%)
  local copies, waits for them, and re-layouts  17.2 us (4%)
  between operations  15.1 us (4%)
  starting transfers between devices  7.21 us (2%)
    psum x1, waiting for transfers between devices, finish(): lax.psum((joined, outproj_term.astype(jnp.bfloat16)), 'seq')  96 us
    all_gather x1, waiting for transfers between devices, on_device(): state_grads = lax.all_gather(state_grad.astype(jnp.bfloat16), 'seq')  51.3 us
    all_gather x1, waiting for transfers between devices, on_device(): inproj_full = lax.all_gather(inproj[0], 'fsdp', axis=0, tiled=True)  34.4 us
    all_gather x1, waiting for transfers between devices, on_device(): states = lax.all_gather(final_state.astype(jnp.bfloat16), 'seq')  33.2 us
    all_gather x1, blocking collectives, on_device(): totals = lax.all_gather(total_log, 'seq')  21 us
    all_gather x1, waiting for transfers between devices, on_device(): outproj_full = lax.all_gather(outproj[0], 'fsdp', axis=0, tiled=True)  14.8 us
    all_gather x1, blocking collectives, finish(): outer_all = lax.all_gather(cotangent[0], 'fsdp')  13.5 us
    dot_general x3, matrix products, section_one(): jnp.einsum('khts,kshp->kthp', decay_mat, head_input, precision=highest)  9.44 us
  transfers between devices with their start and end apart: 9, of which 5 were waited for; matrix products, arithmetic and copies ran while one was open for 16% of the time, Pallas kernels for 0%

profile of v1, /device:TPU:0, one launch (start us, length us, event | category | flops | bytes accessed | tf_op | source)
XLA Modules:
  0.0 409.9 jit_solution(10707965243586987749)
XLA Ops:
  8.7 4.9 %collective-permute-start = (bf16[3,768]{1,0:T(4,128)(2,1)S(1)}, bf16[3,768]{1,0:T(4,128)(2,1)S(1)}, u32[]{:S(2)}, u32[]{:S(2)}) collective-permute-start(bf16[3,768]{1,0:T(4,128)(2,1)S(1)} %slice_bitcast_fusion.1), channel_id=1, source_target_pairs={{0,4},{4,8},{8,12},{12,16},{16,20},{20,24},{24,28},{1,5},{5,9},{9,... | collective-permute-start | bytes 13832 | tf_op jit(solution)/shard_map/ppermute | solution.py:23
  16.0 1.7 fusion.78
  18.7 34.4 %all-gather.15.cloned.1.call-done = bf16[1,768,3352]{2,1,0:T(8,128)(2,1)} async-done(((bf16[1,192,3352]{2,1,0:T(8,128)(2,1)}), bf16[1,768,3352]{2,1,0:T(8,128)(2,1)}) %all-gather.15.cloned.1.call-update) | async-done | bytes 5148688 | tf_op jit(solution)/shard_map/all_gather | solution.py:123
  53.1 4.8 %fusion.4 = f32[136,3352]{0,1:T(8,128)S(1)} fusion(bf16[1,768,3352]{2,1,0:T(8,128)(2,1)} %all-gather.15.cloned.1.call-done, bf16[3,768]{1,0:T(4,128)(2,1)S(1)} %fusion.116, bf16[128,768]{1,0:T(8,128)(2,1)} %fusion.78), kind=kOutput, calls=%fused_computation.6 | convolution fusion | flops 700846080 | bytes 7173376 | tf_op jit(solution)/shard_map/dot_general | solution.py:129
  59.0 1.2 slice.118
  62.7 6.7 %fusion.55 = (f32[128,1792]{0,1:T(8,128)S(1)}, f32[128,1792]{0,1:T(8,128)}) fusion(f32[128,1792]{0,1:T(8,128)} %slice.119, f32[1792]{0:T(1024)S(1)} %get-tuple-element.26, f32[3,1792]{0,1:T(8,128)} %slice.118, f32[1792]{0:T(1024)S(1)} %get-tuple-element.27, f32[1792]{0:T(1024)S(1)} %get-tuple-element.25, f32[1792]{0:T(1024)S(1)} %get-tuple-element.24, ...), kind=kLoop, calls=%fused_computation.68 | loop fusion | flops 3440640 | bytes 2809856 | tf_op jit(solution)/shard_map/jvp(jit(silu))/mul | solution.py:56
  70.6 1.5 convolution_convert_fusion.1
  74.3 21.0 %all-gather.1 = f32[8,1,24]{2,1,0:T(1,128)S(1)} all-gather(f32[1,1,24]{2,1,0:T(1,128)} %get-tuple-element.54), channel_id=3, replica_groups=mesh['seq'=8,'fsdp'=4] {'seq'}, dimensions={0}, use_global_device_ids=true | all-gather | bytes 864 | tf_op jit(solution)/shard_map/all_gather | solution.py:140
  95.3 1.4 select_reduce_fusion
  96.7 1.3 exponential_select_fusion.1
  98.0 1.2 fusion.108
  99.2 33.2 %all-gather.17.cloned.1.call-done = bf16[192,64,128]{2,1,0:T(8,128)(2,1)} async-done(((bf16[24,64,128]{2,1,0:T(8,128)(2,1)}), bf16[192,64,128]{2,1,0:T(8,128)(2,1)}) %all-gather.17.cloned.1.call-update) | async-done | bytes 3145744 | tf_op jit(solution)/shard_map/all_gather | solution.py:141
  132.4 2.7 fusion.1
  135.1 1.7 fusion.102
  136.8 3.3 fusion.30
  140.1 1.2 multiply_reduce_fusion.12
  141.9 14.8 %all-gather.19.cloned.1.call-done = bf16[1,1536,768]{2,1,0:T(8,128)(2,1)} async-done(((bf16[1,384,768]{2,1,0:T(8,128)(2,1)}), bf16[1,1536,768]{2,1,0:T(8,128)(2,1)}) %all-gather.19.cloned.1.call-update) | async-done | bytes 2359312 | tf_op jit(solution)/shard_map/all_gather | solution.py:134
  156.7 2.9 multiply_reduce_fusion.8
  159.7 3.6 multiply_reduce_fusion.7
  163.3 1.6 convolution_convert_fusion
  165.4 4.3 %fusion.50 = (f32[24,128]{1,0:T(8,128)}, f32[24,128]{1,0:T(8,128)}, f32[24,128]{1,0:T(8,128)}, f32[128,128]{1,0:T(8,128)S(1)}) fusion(f32[24,128]{1,0:T(8,128)S(1)} %copy-done.34, f32[128,128]{1,0:T(8,128)S(1)} %fusion.108, f32[24,128]{1,0:T(8,128)S(1)} %copy.120, pred[128,128]{1,0:T(8,128)(4,1)S(1)} %copy-done.32, f32[24,64,128]{2,1,0:T(8,128)S(1)} %bitcast.238, ...), kind=kOutput, calls=%fused_computation.57 | convolution fusion | flops 307076096 | bytes 1781760 | tf_op jit(solution)/shard_map/transpose(jvp(khts,kshp->kthp))/dot_general | solution.py:71
  169.6 1.1 convolution_bitcast_fusion.5
  172.0 1.4 fusion.48
  173.8 51.3 %all-gather.21.cloned.1.call-done = bf16[192,64,128]{2,1,0:T(8,128)(2,1)} async-done(((bf16[24,64,128]{2,1,0:T(8,128)(2,1)}), bf16[192,64,128]{2,1,0:T(8,128)(2,1)}) %all-gather.21.cloned.1.call-update) | async-done | bytes 3145744 | tf_op jit(solution)/shard_map/all_gather | solution.py:168
  225.1 2.6 fusion
  227.7 1.7 multiply_reduce_fusion.6
  229.5 1.9 fusion.33
  231.4 1.4 fusion.47
  232.9 3.9 multiply_reduce_fusion.4
  236.8 1.3 broadcast_multiply_fusion
  238.1 1.5 pad_add_fusion
  239.6 1.2 copy-done.14
  241.8 1.5 copy.138
  243.3 1.6 collective-permute-start.1
  246.5 1.1 reduce_window_sum.25
  248.6 1.8 split.8
  251.5 2.4 add_convert_fusion
  254.1 8.6 %all-gather.5 = bf16[3072,128]{0,1:T(8,128)(2,1)S(1)} all-gather(bf16[768,128]{0,1:T(8,128)(2,1)S(1)} %fusion.155), channel_id=7, replica_groups=mesh['seq'=8,'fsdp'=4] {'fsdp'}, dimensions={0}, use_global_device_ids=true | all-gather | bytes 983040 | tf_op jit(solution)/shard_map/all_gather | solution.py:196
  262.8 1.2 copy.164
  263.9 13.5 %all_gather.56 = bf16[4,128,768]{2,1,0:T(8,128)(2,1)S(1)} all-gather(bf16[1,128,768]{2,1,0:T(8,128)(2,1)S(1)} %copy-done.21), channel_id=1, replica_groups=mesh['seq'=8,'fsdp'=4] {'fsdp'}, dimensions={0}, use_global_device_ids=true | all-gather | bytes 983040 | tf_op jit(solution)/shard_map/all_gather | solution.py:198
  277.6 2.4 fusion.36
  280.2 4.2 %fusion.79 = (f32[768]{0:T(1024)S(1)}, f32[128]{0:T(128)S(1)}, f32[128,768]{1,0:T(8,128)S(1)}) fusion(bf16[1,128,768]{2,1,0:T(8,128)(2,1)S(1)} %copy-done.15, f32[128]{0:T(128)S(1)} %copy-done.42, f32[768]{0:T(1024)S(1)} %reduce.17, bf16[128,3352]{0,1:T(8,128)(2,1)S(1)} %copy-done.13, bf16[1,768,3352]{2,1,0:T(8,128)(2,1)} %all-gather.15.cloned.1.call-done), kind=kOutput, calls=%fused_computation.114 | convolution fusion | flops 659717248 | bytes 6603776 | tf_op jit(solution)/shard_map/dot_general | solution.py:202
  284.5 5.6 %all_gather.53 = f32[4,96,128]{2,1,0:T(8,128)S(1)} all-gather(f32[1,96,128]{2,1,0:T(8,128)S(1)} %bitcast.253), channel_id=1, replica_groups=mesh['seq'=8,'fsdp'=4] {'fsdp'}, dimensions={0}, use_global_device_ids=true | all-gather | bytes 245760 | tf_op jit(solution)/shard_map/all_gather | solution.py:211
  290.3 3.4 fusion.6
  293.7 1.2 pad_maximum_fusion
  294.9 3.1 fusion.43
  298.9 96.0 %all-reduce.22.cloned.1.call-done = (bf16[196,3352]{1,0:T(8,128)(2,1)}, bf16[1,384,768]{2,1,0:T(8,128)(2,1)}) async-done(((bf16[196,3352]{1,0:T(8,128)(2,1)}, bf16[1,384,768]{2,1,0:T(8,128)(2,1)}), (bf16[196,3352]{1,0:T(8,128)(2,1)}, bf16[1,384,768]{2,1,0:T(8,128)(2,1)})) %all-reduce.22.cloned.1.call-update) | async-done | bytes 1903824 | tf_op jit(solution)/shard_map/psum | solution.py:215
  394.9 3.1 fusion.19
  (215 shorter events, 25.5 us)
Async XLA Ops:
  7.2 10.5 %copy-start.36 = (f32[1,4,1792]{2,1,0:T(4,128)S(1)}, f32[1,4,1792]{2,1,0:T(4,128)}, u32[]{:S(2)}) copy-start(f32[1,4,1792]{2,1,0:T(4,128)} %param.17) | copy-start | bytes 86020
  7.2 10.6 %copy-start.47 = (f32[1,1792]{1,0:T(1,128)S(1)}, f32[1,1792]{1,0:T(1,128)}, u32[]{:S(2)}) copy-start(f32[1,1792]{1,0:T(1,128)} %param.18) | copy-start | bytes 21508
  7.2 45.9 %all-gather.15.cloned.1.call-start = ((), (), s32[]{:S(2)}) async-start(), calls=%async_computation | async-start | bytes 6635520 | tf_op jit(solution)/shard_map/all_gather | solution.py:123
  7.9 124.4 %all-gather.17.cloned.1.call-start = ((), (), s32[]{:S(2)}) async-start(), calls=%async_computation.1 | async-start | bytes 3538944 | tf_op jit(solution)/shard_map/all_gather | solution.py:141
  8.7 9.8 %collective-permute-start = (bf16[3,768]{1,0:T(4,128)(2,1)S(1)}, bf16[3,768]{1,0:T(4,128)(2,1)S(1)}, u32[]{:S(2)}, u32[]{:S(2)}) collective-permute-start(bf16[3,768]{1,0:T(4,128)(2,1)S(1)} %slice_bitcast_fusion.1), channel_id=1, source_target_pairs={{0,4},{4,8},{8,12},{12,16},{16,20},{20,24},{24,28},{1,5},{5,9},{9,... | collective-permute-start | bytes 13832 | tf_op jit(solution)/shard_map/ppermute | solution.py:23
  16.0 44.2 %copy-start.51 = (f32[24]{0:T(128)}, f32[24]{0:T(128)S(1)}, u32[]{:S(2)}) copy-start(f32[24]{0:T(128)S(1)} %bitcast_negate_fusion) | copy-start | bytes 292
  17.8 44.9 %copy-start.25 = (f32[1792]{0:T(1024)}, f32[1792]{0:T(1024)S(1)}, u32[]{:S(2)}) copy-start(f32[1792]{0:T(1024)S(1)} %get-tuple-element.25) | copy-start | bytes 21508
  17.8 44.9 %copy-start.27 = (f32[1792]{0:T(1024)}, f32[1792]{0:T(1024)S(1)}, u32[]{:S(2)}) copy-start(f32[1792]{0:T(1024)S(1)} %get-tuple-element.26) | copy-start | bytes 21508
  17.8 44.9 %copy-start.29 = (f32[1792]{0:T(1024)}, f32[1792]{0:T(1024)S(1)}, u32[]{:S(2)}) copy-start(f32[1792]{0:T(1024)S(1)} %get-tuple-element.27) | copy-start | bytes 21508
  57.9 82.2 %copy-start = (f32[136,3352]{0,1:T(8,128)}, f32[136,3352]{0,1:T(8,128)S(1)}, u32[]{:S(2)}) copy-start(f32[136,3352]{0,1:T(8,128)S(1)} %fusion.4) | copy-start | bytes 5470468
  62.7 6.8 %copy-start.45 = (f32[24]{0:T(128)}, f32[24]{0:T(128)S(1)}, u32[]{:S(2)}) copy-start(f32[24]{0:T(128)S(1)} %get-tuple-element.53) | copy-start | bytes 292
  72.2 84.5 %all-gather.19.cloned.1.call-start = ((), (), s32[]{:S(2)}) async-start(), calls=%async_computation.2 | async-start | bytes 2949120 | tf_op jit(solution)/shard_map/all_gather | solution.py:134
  72.9 152.1 %all-gather.21.cloned.1.call-start = ((), (), s32[]{:S(2)}) async-start(), calls=%async_computation.3 | async-start | bytes 3538944 | tf_op jit(solution)/shard_map/all_gather | solution.py:168
  132.4 4.4 %copy-start.3 = (f32[128,1536]{0,1:T(8,128)S(1)}, f32[128,1536]{0,1:T(8,128)}, u32[]{:S(2)}) copy-start(f32[128,1536]{0,1:T(8,128)} %copy-done.2) | copy-start | bytes 2359300
  132.4 4.4 %copy-start.23 = (f32[128,24]{0,1:T(8,128)S(1)}, f32[128,24]{0,1:T(8,128)}, u32[]{:S(2)}) copy-start(f32[128,24]{0,1:T(8,128)} %get-tuple-element.58) | copy-start | bytes 36868
  132.4 4.4 %copy-start.31 = (pred[128,128]{1,0:T(8,128)(4,1)S(1)}, pred[128,128]{1,0:T(8,128)(4,1)}, u32[]{:S(2)}) copy-start(pred[128,128]{1,0:T(8,128)(4,1)} %iota_compare_fusion.1) | copy-start | bytes 49156
  132.4 4.4 %copy-start.33 = (f32[24,128]{1,0:T(8,128)S(1)}, f32[24,128]{1,0:T(8,128)}, u32[]{:S(2)}) copy-start(f32[24,128]{1,0:T(8,128)} %get-tuple-element.45) | copy-start | bytes 36868
  132.4 4.5 %copy-start.61 = (f32[1,24]{1,0:T(1,128)S(1)}, f32[1,24]{1,0:T(1,128)}, u32[]{:S(2)}) copy-start(f32[1,24]{1,0:T(1,128)} %param.21) | copy-start | bytes 292
  135.1 5.0 %copy-start.5 = (f32[24,64,128]{2,1,0:T(8,128)}, f32[24,64,128]{2,1,0:T(8,128)S(1)}, u32[]{:S(2)}) copy-start(f32[24,64,128]{2,1,0:T(8,128)S(1)} %fusion.1) | copy-start | bytes 2359300
  136.8 4.6 %copy-start.19 = (f32[128,24,64]{0,2,1:T(8,128)}, f32[128,24,64]{0,2,1:T(8,128)S(1)}, u32[]{:S(2)}) copy-start(f32[128,24,64]{0,2,1:T(8,128)S(1)} %fusion.102) | copy-start | bytes 2359300
  141.9 17.7 %copy-start.49 = (f32[128]{0:T(128)}, f32[128]{0:T(128)S(1)}, u32[]{:S(2)}) copy-start(f32[128]{0:T(128)S(1)} %fusion.130) | copy-start | bytes 1540
  159.7 5.5 %copy-start.53 = (f32[1,24]{1,0:T(1,128)S(1)}, f32[1,24]{1,0:T(1,128)}, u32[]{:S(2)}) copy-start(f32[1,24]{1,0:T(1,128)} %get-tuple-element.52) | copy-start | bytes 292
  159.7 5.6 %copy-start.37 = (f32[8,24]{1,0:T(8,128)S(1)}, f32[8,24]{1,0:T(8,128)}, u32[]{:S(2)}) copy-start(f32[8,24]{1,0:T(8,128)} %get-tuple-element.28) | copy-start | bytes 2308
  159.7 5.6 %copy-start.55 = (pred[8]{0:T(512)(128)(4,1)S(1)}, pred[8]{0:T(512)(128)(4,1)}, u32[]{:S(2)}) copy-start(pred[8]{0:T(512)(128)(4,1)} %copy-done.54) | copy-start | bytes 28
  159.7 5.6 %copy-start.4 = (f32[128,1536]{0,1:T(8,128)S(1)}, f32[128,1536]{0,1:T(8,128)}, u32[]{:S(2)}) copy-start(f32[128,1536]{0,1:T(8,128)} %copy-done.2) | copy-start | bytes 2359300
  159.7 5.6 %copy-start.32 = (pred[128,128]{1,0:T(8,128)(4,1)S(1)}, pred[128,128]{1,0:T(8,128)(4,1)}, u32[]{:S(2)}) copy-start(pred[128,128]{1,0:T(8,128)(4,1)} %iota_compare_fusion.1) | copy-start | bytes 49156
  159.7 5.6 %copy-start.34 = (f32[24,128]{1,0:T(8,128)S(1)}, f32[24,128]{1,0:T(8,128)}, u32[]{:S(2)}) copy-start(f32[24,128]{1,0:T(8,128)} %get-tuple-element.45) | copy-start | bytes 36868
  164.9 112.8 %all-gather.25.cloned.1.call-start = ((), (), s32[]{:S(2)}) async-start(), calls=%async_computation.5 | async-start | bytes 1966080 | tf_op jit(solution)/shard_map/all_gather | solution.py:197
  165.3 5.4 %copy-start.20 = (f32[128,24,64]{0,2,1:T(8,128)S(1)}, f32[128,24,64]{0,2,1:T(8,128)}, u32[]{:S(2)}) copy-start(f32[128,24,64]{0,2,1:T(8,128)} %copy-done.19) | copy-start | bytes 2359300
  173.5 116.8 %all-gather.23.cloned.1.call-start = ((), (), s32[]{:S(2)}) async-start(), calls=%async_computation.4 | async-start | bytes 4290560 | tf_op jit(solution)/shard_map/all_gather | solution.py:195
  227.7 3.7 copy-start.7
  232.9 3.9 copy-start.26
  232.9 3.9 copy-start.28
  232.9 3.9 copy-start.30
  240.8 4.1 %copy-start.44 = (f32[1,24]{1,0:T(1,128)S(1)}, f32[1,24]{1,0:T(1,128)}, u32[]{:S(2)}) copy-start(f32[1,24]{1,0:T(1,128)} %param.19) | copy-start | bytes 292
  240.8 4.1 %copy-start.46 = (f32[24]{0:T(128)S(1)}, f32[24]{0:T(128)}, u32[]{:S(2)}) copy-start(f32[24]{0:T(128)} %copy-done.45) | copy-start | bytes 292
  240.8 5.1 %copy-start.8 = (f32[24,64,128]{2,1,0:T(8,128)S(1)}, f32[24,64,128]{2,1,0:T(8,128)}, u32[]{:S(2)}) copy-start(f32[24,64,128]{2,1,0:T(8,128)} %copy-done.7) | copy-start | bytes 2359300
  241.8 4.5 %copy-start.39 = (f32[24,128]{1,0:T(8,128)S(1)}, f32[24,128]{1,0:T(8,128)}, u32[]{:S(2)}) copy-start(f32[24,128]{1,0:T(8,128)} %get-tuple-element.14) | copy-start | bytes 36868
  241.8 4.5 %copy-start.40 = (f32[24,128]{1,0:T(8,128)S(1)}, f32[24,128]{1,0:T(8,128)}, u32[]{:S(2)}) copy-start(f32[24,128]{1,0:T(8,128)} %get-tuple-element.15) | copy-start | bytes 36868
  241.8 5.9 %copy-start.38 = (f32[24,128]{1,0:T(8,128)S(1)}, f32[24,128]{1,0:T(8,128)}, u32[]{:S(2)}) copy-start(f32[24,128]{1,0:T(8,128)} %get-tuple-element.16) | copy-start | bytes 36868
  241.8 5.9 %copy-start.52 = (f32[24]{0:T(128)S(1)}, f32[24]{0:T(128)}, u32[]{:S(2)}) copy-start(f32[24]{0:T(128)} %copy-done.51) | copy-start | bytes 292
  243.3 7.1 %collective-permute-start.1 = (f32[3,1792]{1,0:T(4,128)S(1)}, f32[3,1792]{1,0:T(4,128)}, u32[]{:S(2)}, u32[]{:S(2)}) collective-permute-start(f32[3,1792]{1,0:T(4,128)S(1)} %copy.138), channel_id=1, source_target_pairs={{4,0},{8,4},{12,8},{16,12},{20,16},{24,20},{28,24},{5,1},{9,5},{13... | collective-permute-start | bytes 64520 | tf_op jit(solution)/shard_map/ppermute | solution.py:23
  253.9 10.0 %copy-start.21 = (bf16[1,128,768]{2,1,0:T(8,128)(2,1)S(1)}, bf16[1,128,768]{2,1,0:T(8,128)(2,1)}, u32[]{:S(2)}) copy-start(bf16[1,128,768]{2,1,0:T(8,128)(2,1)} %param.12) | copy-start | bytes 589828
  254.0 140.9 %all-reduce.22.cloned.1.call-start = ((), (), s32[]{:S(2)}) async-start(), calls=%async_computation.6 | async-start | bytes 3944448 | tf_op jit(solution)/shard_map/psum | solution.py:215
  254.1 23.3 %copy-start.35 = (f32[1536]{0:T(1024)S(1)}, f32[1536]{0:T(1024)}, u32[]{:S(2)}) copy-start(f32[1536]{0:T(1024)} %get-tuple-element.32) | copy-start | bytes 18436
  263.9 16.2 %copy-start.63 = (f32[1,24]{1,0:T(1,128)S(1)}, f32[1,24]{1,0:T(1,128)}, u32[]{:S(2)}) copy-start(f32[1,24]{1,0:T(1,128)} %param.20) | copy-start | bytes 292
  263.9 16.2 %copy-start.13 = (bf16[128,3352]{0,1:T(8,128)(2,1)S(1)}, bf16[128,3352]{0,1:T(8,128)(2,1)}, u32[]{:S(2)}) copy-start(bf16[128,3352]{0,1:T(8,128)(2,1)} %add_convert_fusion) | copy-start | bytes 2574340
  394.9 4.6 %copy-start.22 = (bf16[1,384,768]{2,1,0:T(8,128)(2,1)S(1)}, bf16[1,384,768]{2,1,0:T(8,128)(2,1)}, u32[]{:S(2)}) copy-start(bf16[1,384,768]{2,1,0:T(8,128)(2,1)} %get-tuple-element.31) | copy-start | bytes 1769476
  (25 other events, 59.3 us)
Sparse Core Ops, SparseCore 0:
  9.6 43.4 all-gather.14
  72.3 60.0 all-gather.16
  133.9 22.7 all-gather.18
  165.0 59.9 all-gather.20
  226.5 18.2 all-gather.24
  254.1 35.8 all-gather.22
  295.0 99.8 all-reduce.21
